TPU v7x, 256 devices: a whole 4x4x8 slice. The times are simulated.
256 devices in a mesh: dp: 32 (over x, z), expert: 8 (over y, core).
Axes of the slice: x: 4, y: 4, z: 8, core: 2. Of those that a mesh axis runs over, the one named last changes fastest.
Arguments:
- text_embed: bfloat16 [16384, 2048], P(('dp', 'expert')), may hold values from -6 to 6
- image_feats: bfloat16 [8192, 4608], P(('dp', 'expert')), may hold values from -6 to 6
- tile_pos: int32 [8192], P(('dp', 'expert')), may hold values from 0 to 16383, as said below
- proj_in: bfloat16 [4608, 2048], P(None, 'expert'), may hold values from -0.09375 to 0.09375
- proj_out: bfloat16 [2048, 2048], P('expert'), may hold values from -0.125 to 0.125
- norm_gain: float32 [2048], replicated, may hold values from 0.1 to 1.9
- shared_gate: bfloat16 [2048, 2816], P(None, 'expert'), may hold values from -0.125 to 0.125
- shared_up: bfloat16 [2048, 2816], P(None, 'expert'), may hold values from -0.125 to 0.125
- shared_down: bfloat16 [2816, 2048], P('expert'), may hold values from -0.109375 to 0.109375
- expert_gate: bfloat16 [32, 2048, 1408], P('dp', None, 'expert'), may hold values from -0.125 to 0.125
- expert_up: bfloat16 [32, 2048, 1408], P('dp', None, 'expert'), may hold values from -0.125 to 0.125
- expert_down: bfloat16 [32, 1408, 2048], P('dp', 'expert'), may hold values from -0.15625 to 0.15625
- route_ids: int32 [16384, 2], P(('dp', 'expert')), may hold values from 0 to 31, all different within a row; in each aligned block of 512 rows (0 to 511, 512 to 1023, ...) at most 48 rows name the same one
- route_wts: int32 [16384, 2], P(('dp', 'expert')), may hold values from 1 to 65535
Outputs:
- block_out: bfloat16 [16384, 2048], P(('dp', 'expert'))
Inputs may be any that keep to these rules, and one draw needn't show every extreme that they name: `tile_pos`: positions are distinct. The 32 image tokens of one device go 1 to each index of dp, always to rows held by the devices with the sender's own index of expert. `route_ids`: in each aligned block of 512 rows no expert is named by more than 48 rows, a bound that some block reaches.
All inputs are finite; a program needn't handle non-finite values.
Results may differ from a plain program's by a relative error of at most 0.018.
Values may be sent and summed in bfloat16 or wider, within the bound.
A program may use at most 128 MiB of HBM per device.

v0:
```python
import jax
import jax.numpy as jnp
from jax import lax
from jax.sharding import PartitionSpec as P


def normalize(rows, norm_gain):
    rows_f = rows.astype(jnp.float32)
    meansq = jnp.mean(rows_f * rows_f, axis=-1, keepdims=True) + 1e-06
    return (rows_f * lax.rsqrt(meansq) * norm_gain).astype(jnp.bfloat16)


def project_part(feats, proj_in, proj_out):
    vis_hidden = jax.nn.gelu(
        jnp.dot(feats, proj_in, preferred_element_type=jnp.float32), approximate=True
    ).astype(jnp.bfloat16)
    return jnp.dot(vis_hidden, proj_out, preferred_element_type=jnp.float32)


def shards(
    text_embed,
    image_feats,
    tile_pos,
    proj_in,
    proj_out,
    norm_gain,
    shared_gate,
    shared_up,
    shared_down,
    expert_gate,
    expert_up,
    expert_down,
    route_ids,
    route_wts,
):
    tok_dev = text_embed.shape[0]
    img_dev = image_feats.shape[0]
    width_model = text_embed.shape[1]
    n_data = lax.axis_size("dp")
    n_group = lax.axis_size("expert")
    peer = img_dev // n_data
    my_place = lax.axis_index("expert")
    owner = tile_pos // tok_dev
    dest_index = owner // n_group
    order = jnp.argsort(dest_index, stable=True)
    sorted_feats = image_feats[order].reshape(n_data, peer, image_feats.shape[1])
    sorted_offs = (tile_pos[order] % tok_dev).reshape(n_data, peer)
    moved_feats, moved_offs = (
        lax.all_to_all(sorted_feats, "dp", split_axis=0, concat_axis=0, tiled=True),
        lax.all_to_all(sorted_offs, "dp", split_axis=0, concat_axis=0, tiled=True),
    )
    moved_feats = moved_feats.reshape(img_dev, image_feats.shape[1])
    moved_offs = moved_offs.reshape(img_dev)
    texts, feats, offsets, ids, weights = (
        lax.all_gather(text_embed, "expert", axis=0, tiled=True),
        lax.all_gather(moved_feats, "expert", axis=0, tiled=True),
        lax.all_gather(moved_offs, "expert", axis=0, tiled=True),
        lax.all_gather(route_ids, "expert", axis=0, tiled=True),
        lax.all_gather(route_wts, "expert", axis=0, tiled=True),
    )
    partial_value = project_part(feats, proj_in, proj_out)
    projected = lax.psum(partial_value.astype(jnp.bfloat16), "expert")
    block_start = jnp.arange(offsets.shape[0], dtype=jnp.int32) // img_dev * tok_dev
    embed_group = texts.at[offsets + block_start].set(projected)
    normed = normalize(embed_group, norm_gain)
    own_rows = lax.dynamic_slice_in_dim(embed_group, my_place * tok_dev, tok_dev, 0)
    gate_s = jnp.dot(normed, shared_gate, preferred_element_type=jnp.float32)
    up_s = jnp.dot(normed, shared_up, preferred_element_type=jnp.float32)
    shared_hidden = (jax.nn.silu(gate_s) * up_s).astype(jnp.bfloat16)
    group_rows = normed.shape[0]
    top_count = ids.shape[1]
    capacity = 3 * group_rows * top_count // (2 * n_data)
    share = capacity // n_group
    flat_ids = ids.reshape(-1)
    onehot = (flat_ids[:, None] == jnp.arange(n_data, dtype=jnp.int32)[None, :]).astype(jnp.int32)
    rank = jnp.sum(jnp.cumsum(onehot, axis=0) * onehot, axis=1) - 1
    pair_token = jnp.arange(group_rows * top_count, dtype=jnp.int32) // top_count
    send = (
        jnp.zeros((n_data, capacity, width_model), jnp.bfloat16)
        .at[flat_ids, rank]
        .set(normed[pair_token])
    )
    slots = lax.all_to_all(send, "dp", split_axis=0, concat_axis=0, tiled=True)
    gate_e = jnp.einsum("ncd,df->ncf", slots, expert_gate[0], preferred_element_type=jnp.float32)
    up_e = jnp.einsum("ncd,df->ncf", slots, expert_up[0], preferred_element_type=jnp.float32)
    hidden_e = (jax.nn.silu(gate_e) * up_e).astype(jnp.bfloat16)
    partial_out = jnp.einsum(
        "ncf,fd->ncd", hidden_e, expert_down[0], preferred_element_type=jnp.float32
    )
    summed = lax.psum_scatter(
        partial_out.astype(jnp.bfloat16), "expert", scatter_dimension=1, tiled=True
    )
    returned = lax.all_to_all(summed, "dp", split_axis=0, concat_axis=0, tiled=True)
    inside = rank // share == my_place
    local_slot = jnp.where(inside, rank - my_place * share, 0)
    picked = returned.reshape(n_data * share, width_model)[flat_ids * share + local_slot]
    weights_f = weights.astype(jnp.float32)
    weights_n = weights_f / jnp.sum(weights_f, axis=1, keepdims=True)
    coef = jnp.where(inside, weights_n.reshape(-1), 0.0)
    combined = jnp.sum(
        (picked.astype(jnp.float32) * coef[:, None]).reshape(group_rows, top_count, width_model),
        axis=1,
    )
    total = lax.psum_scatter(
        (jnp.dot(shared_hidden, shared_down, preferred_element_type=jnp.float32) + combined).astype(
            jnp.bfloat16
        ),
        "expert",
        scatter_dimension=0,
        tiled=True,
    ).astype(jnp.float32)
    return (own_rows.astype(jnp.float32) + total).astype(jnp.bfloat16)


def solution(mesh):
    return jax.shard_map(
        shards,
        mesh=mesh,
        in_specs=(
            P(("dp", "expert"), None),
            P(("dp", "expert"), None),
            P(("dp", "expert")),
            P(None, "expert"),
            P("expert", None),
            P(),
            P(None, "expert"),
            P(None, "expert"),
            P("expert", None),
            P("dp", None, "expert"),
            P("dp", None, "expert"),
            P("dp", "expert", None),
            P(("dp", "expert"), None),
            P(("dp", "expert"), None),
        ),
        out_specs=P(("dp", "expert"), None),
        check_vma=False,
    )
```

profile of v0, /device:TPU:2, one launch (start us, length us, event | category | flops | bytes accessed | tf_op | source)
XLA Modules:
  0.0 534.1 jit_solution(12676066431425173796)
XLA Ops:
  6.5 0.8 and_select_fusion.4
  7.4 1.6 sort.17
  9.0 2.0 gather_fusion.1
  11.0 0.5 broadcast.394
  11.5 0.8 reduce.7
  12.4 0.1 reshape.350
  12.4 23.1 %all_to_all.21 = bf16[32,2,2304]{2,1,0:T(2,128)(2,1)S(1)} all-to-all(bf16[32,2,2304]{2,1,0:T(2,128)(2,1)S(1)} %reshape.350), channel_id=1, replica_groups=mesh['dp'=32,'expert'=8] {'dp'}, dimensions={0} | all-to-all | bytes 589824 | tf_op jit(solution)/shard_map/all_to_all | solution.py:49
  35.6 0.2 reshape.351
  35.9 0.8 copy.50
  36.6 0.0 all-gather.7.cloned.1.call-start
  36.7 0.7 all-gather.7.cloned.1.call-update
  37.4 0.7 gather_fusion
  38.1 0.7 copy.48
  38.8 5.8 %all-to-all-start = ((s32[32,1,1]{2,1,0:T(1,128)}), s32[32,1,1]{2,1,0:T(1,128)S(1)}, u32[]{:S(2)}, u32[]{:S(2)}) async-start(s32[32,1,1]{2,1,0:T(1,128)} %copy.48), calls=%async_computation | async-start | bytes 32768 | tf_op jit(solution)/shard_map/all_to_all | solution.py:50
  44.6 0.0 all-reduce.3.cloned.1.call-start
  44.7 10.8 %all-gather.2 = s32[8,64,2]{1,2,0:T(2,128)S(1)} all-gather(s32[1,64,2]{1,2,0:T(2,128)S(1)} %bitcast.70), channel_id=1, replica_groups=mesh['dp'=32,'expert'=8] {'expert'}, dimensions={0}, use_global_device_ids=true | all-gather | bytes 4608 | tf_op jit(solution)/shard_map/all_gather | solution.py:58
  55.5 0.1 copy.53
  55.6 0.2 copy.51
  55.8 0.2 eq.47
  56.0 0.2 reshape.266
  56.2 9.0 %reduce-window.6 = s32[32,8,128]{2,1,0:T(8,128)S(1)} reduce-window(s32[32,8,128]{2,1,0:T(8,128)S(1)} %fusion.38, s32[]{:T(128)} %constant.99.clone.1), window={size=1x1x128 pad=0_0x0_0x127_0}, to_apply=%region_4.5 | reduce-window | flops 4161536 | bytes 262148 | tf_op jit(solution)/shard_map/reduce-window
  65.3 0.1 slice.16
  65.3 0.1 copy.55
  65.5 0.1 copy.56
  65.6 0.1 broadcast_add_fusion
  65.8 0.1 multiply_reduce_fusion.1
  65.9 0.1 and_reduce_fusion
  66.0 0.0 all-gather.9.cloned.1.call-done
  66.1 4.6 convolution_convert_fusion.1
  70.7 0.0 reduce-scatter.3.cloned.1.call-start
  70.7 0.7 dynamic-slice
  72.1 0.7 reduce.3
  72.8 0.2 dynamic-update-slice
  73.0 6.7 %all-reduce = s32[256]{0:T(256)S(1)} all-reduce(s32[256]{0:T(256)S(1)} %dynamic-update-slice), channel_id=2, replica_groups=mesh['dp'=32,'expert'=8] {'expert'}, use_global_device_ids=true, to_apply=%add | all-reduce | flops 256 | bytes 2048 | tf_op jit(solution)/shard_map/all_gather | solution.py:57
  79.8 12.6 %all-gather.7.cloned.1.call-done = bf16[512,2048]{1,0:T(8,128)(2,1)} async-done(((bf16[64,2048]{1,0:T(8,128)(2,1)}), bf16[512,2048]{1,0:T(8,128)(2,1)}) %all-gather.7.cloned.1.call-update) | async-done | bytes 2097168 | tf_op jit(solution)/shard_map/all_gather | solution.py:55
  92.3 70.3 %all-reduce.3.cloned.1.call-done = bf16[256,2048]{1,0:T(8,128)(2,1)} async-done(((bf16[256,2048]{1,0:T(8,128)(2,1)}), bf16[256,2048]{1,0:T(8,128)(2,1)}) %all-reduce.3.cloned.1.call-update) | async-done | bytes 1048592 | tf_op jit(solution)/shard_map/psum | solution.py:62
  162.6 6.4 %scatter_fusion = bf16[512,2048]{1,0:T(8,128)(2,1)} fusion(bf16[512,2048]{1,0:T(8,128)(2,1)} %all-gather.7.cloned.1.call-done, s32[256]{0:T(256)S(1)} %compare_select_fusion.5, bf16[256,2048]{1,0:T(8,128)(2,1)} %all-reduce.3.cloned.1.call-done), kind=kCustom, calls=%fused_computation.4 | custom fusion | bytes 3146752 | tf_op jit(solution)/shard_map/scatter | solution.py:64
  169.1 2.2 fusion
  171.3 1.9 fusion.2
  173.2 22.1 %scatter_custom_fusion.1 = bf16[1536,2048]{1,0:T(8,128)(2,1)} fusion(s32[1024]{0:T(1024)S(1)} %get-tuple-element.14, bf16[512,2048]{1,0:T(8,128)(2,1)} %fusion.2, s32[1024]{0:T(1024)S(1)} %get-tuple-element.13, bf16[]{:T(256)} %constant.118.clone.1), kind=kCustom, calls=%fused_computation.13 | custom fusion | bytes 6291968
  195.3 146.9 %all_to_all.22 = bf16[32,48,2048]{2,1,0:T(8,128)(2,1)S(1)} all-to-all(bf16[32,48,2048]{2,1,0:T(8,128)(2,1)} %bitcast.61), channel_id=1, replica_groups=mesh['dp'=32,'expert'=8] {'dp'}, dimensions={0} | all-to-all | bytes 12582912 | tf_op jit(solution)/shard_map/all_to_all | solution.py:83
  342.2 2.7 copy-done.4
  344.9 3.0 fusion.13
  347.9 12.3 %convolution_convert_fusion = bf16[32,48,2048]{2,1,0:T(8,128)(2,1)} fusion(f32[32,48,176]{2,1,0:T(8,128)} %fusion.13, bf16[32,48,2048]{2,1,0:T(8,128)(2,1)} %copy-done.4, bf16[1,176,2048]{2,1,0:T(8,128)(2,1)S(1)} %copy-done.11, bf16[1,2048,176]{1,2,0:T(8,128)(2,1)S(1)} %copy-done.12), kind=kOutput, calls=%fused_computation.9 | convolution fusion | flops 2219360256 | bytes 15106048 | tf_op jit(solution)/shard_map/ncf,fd->ncd/dot_general | solution.py:87
  360.3 8.9 %copy.57 = bf16[32,48,2048]{2,0,1:T(8,128)(2,1)} copy(bf16[32,48,2048]{2,1,0:T(8,128)(2,1)} %convolution_convert_fusion) | data formatting | bytes 12582912 | tf_op jit(solution)/shard_map/convert_element_type | solution.py:91
  369.2 44.5 %reduce-scatter.3.cloned.1.call-done = bf16[32,6,2048]{2,0,1:T(8,128)(2,1)} async-done(((bf16[32,48,2048]{2,0,1:T(8,128)(2,1)}), bf16[32,6,2048]{2,0,1:T(8,128)(2,1)}) %reduce-scatter.3.cloned.1.call-update) | async-done | bytes 786448 | tf_op jit(solution)/shard_map/reduce_scatter | solution.py:90
  413.7 2.6 copy.58
  416.2 10.1 %all-to-all-start.3 = ((bf16[32,6,2048]{2,1,0:T(8,128)(2,1)}), bf16[32,6,2048]{2,1,0:T(8,128)(2,1)S(1)}, u32[]{:S(2)}, u32[]{:S(2)}) async-start(bf16[32,6,2048]{2,1,0:T(8,128)(2,1)} %copy.58), calls=%async_computation.4 | async-start | bytes 2097152 | tf_op jit(solution)/shard_map/all_to_all | solution.py:93
  426.4 0.3 reduce-scatter.5.cloned.1.call-start
  426.6 0.2 div.94
  426.9 0.3 and.78
  427.1 8.6 %all-gather.3 = s32[8,64,2]{1,2,0:T(2,128)S(1)} all-gather(s32[1,64,2]{1,2,0:T(2,128)S(1)} %bitcast.71), channel_id=1, replica_groups=mesh['dp'=32,'expert'=8] {'expert'}, dimensions={0}, use_global_device_ids=true | all-gather | bytes 4608 | tf_op jit(solution)/shard_map/all_gather | solution.py:59
  435.8 0.2 copy.61
  436.0 0.1 reshape.339
  436.0 0.1 fusion.31
  436.2 2.9 fusion.50
  439.1 13.1 %all-to-all-done.3 = bf16[32,6,2048]{2,1,0:T(8,128)(2,1)S(1)} async-done(((bf16[32,6,2048]{2,1,0:T(8,128)(2,1)}), bf16[32,6,2048]{2,1,0:T(8,128)(2,1)S(1)}, u32[]{:S(2)}, u32[]{:S(2)}) %all-to-all-start.3) | async-done | bytes 786464 | tf_op jit(solution)/shard_map/all_to_all | solution.py:93
  452.2 0.3 reshape.268
  452.4 6.1 %gather_fusion.2 = bf16[1024,2048]{1,0:T(8,128)(2,1)} fusion(bf16[192,2048]{1,0:T(8,128)(2,1)S(1)} %reshape.268, s32[1024]{0:T(1024)S(1)} %broadcast_clamp_fusion), kind=kCustom, calls=%fused_computation.3 | custom fusion | bytes 8392704 | tf_op jit(solution)/shard_map/gather | solution.py:96
  458.5 9.6 %reshape.273 = f32[512,2,2048]{2,1,0:T(2,128)} reshape(bf16[1024,2048]{1,0:T(8,128)(2,1)} %gather_fusion.2) | data formatting | bytes 12582912 | tf_op jit(solution)/shard_map/convert_element_type | solution.py:101
  468.2 15.5 %multiply_reduce_fusion = f32[512,2048]{1,0:T(8,128)} fusion(f32[512,2,2048]{2,1,0:T(2,128)} %reshape.273, f32[512,2]{1,0:T(8,128)S(1)} %fusion.31), kind=kLoop, calls=%fused_computation.6 | loop fusion | flops 3145728 | bytes 12587008 | tf_op jit(solution)/shard_map/reduce_sum | solution.py:100
  483.6 7.4 %add_convert_fusion = bf16[512,2048]{1,0:T(8,128)(2,1)} fusion(f32[512,2048]{1,0:T(8,128)} %multiply_reduce_fusion, bf16[352,2048]{1,0:T(8,128)(2,1)} %param.22, bf16[512,2048]{1,0:T(8,128)(2,1)} %fusion.2, bf16[2048,352]{0,1:T(8,128)(2,1)} %param.21, f32[512,352]{0,1:T(8,128)S(1)} %fusion.50), kind=kOutput, calls=%fused_computation.15 | convolution fusion | flops 1479573504 | bytes 11993088 | tf_op jit(solution)/shard_map/dot_general | solution.py:105
  491.1 34.4 %reduce-scatter.5.cloned.1.call-done = bf16[64,2048]{1,0:T(8,128)(2,1)} async-done(((bf16[512,2048]{1,0:T(8,128)(2,1)}), bf16[64,2048]{1,0:T(8,128)(2,1)}) %reduce-scatter.5.cloned.1.call-update) | async-done | bytes 262160 | tf_op jit(solution)/shard_map/reduce_scatter | solution.py:104
  525.5 1.8 add_convert_fusion.1
  (53 shorter events, 0.4 us)
Async XLA Ops:
  6.5 59.5 %copy-start = (bf16[4608,256]{1,0:T(8,128)(2,1)S(1)}, bf16[4608,256]{1,0:T(8,128)(2,1)}, u32[]{:S(2)}) copy-start(bf16[4608,256]{1,0:T(8,128)(2,1)} %param.17) | copy-start | bytes 7077892
  6.5 59.5 %all-gather.9.cloned.1.call-start = ((), (), s32[]{:S(2)}) async-start(), calls=%async_computation.10 | async-start | bytes 2654208 | tf_op jit(solution)/shard_map/all_gather | solution.py:56
  11.0 26.4 %copy-start.2 = (s32[32]{0:T(128)S(1)}, s32[32]{0:T(128)}, u32[]{:S(2)}) copy-start(s32[32]{0:T(128)} %param.16) | copy-start | bytes 388
  11.0 33.7 %copy-start.6 = (s32[64,2]{0,1:T(2,128)S(1)}, s32[64,2]{0,1:T(2,128)}, u32[]{:S(2)}) copy-start(s32[64,2]{0,1:T(2,128)} %param.26) | copy-start | bytes 1540
  35.8 30.0 %copy-start.9 = (s32[2]{0:T(128)S(1)}, s32[2]{0:T(128)}, u32[]{:S(2)}) copy-start(s32[2]{0:T(128)} %constant.129) | copy-start | bytes 28
  35.8 30.1 %copy-start.8 = (s32[2]{0:T(128)S(1)}, s32[2]{0:T(128)}, u32[]{:S(2)}) copy-start(s32[2]{0:T(128)} %constant.132) | copy-start | bytes 28
  36.6 55.7 %all-gather.7.cloned.1.call-start = ((), (), s32[]{:S(2)}) async-start(), calls=%async_computation.6 | async-start | bytes 2359296 | tf_op jit(solution)/shard_map/all_gather | solution.py:55
  38.8 33.3 %all-to-all-start = ((s32[32,1,1]{2,1,0:T(1,128)}), s32[32,1,1]{2,1,0:T(1,128)S(1)}, u32[]{:S(2)}, u32[]{:S(2)}) async-start(s32[32,1,1]{2,1,0:T(1,128)} %copy.48), calls=%async_computation | async-start | bytes 32768 | tf_op jit(solution)/shard_map/all_to_all | solution.py:50
  44.6 118.0 %all-reduce.3.cloned.1.call-start = ((), (), s32[]{:S(2)}) async-start(), calls=%async_computation.7 | async-start | bytes 2097152 | tf_op jit(solution)/shard_map/psum | solution.py:62
  66.0 4.7 copy-start.13
  70.7 343.0 %reduce-scatter.3.cloned.1.call-start = ((), (), s32[]{:S(2)}) async-start(), calls=%async_computation.8 | async-start | bytes 7077888 | tf_op jit(solution)/shard_map/reduce_scatter | solution.py:90
  79.8 91.6 %copy-start.5 = (f32[2048]{0:T(1024)S(1)}, f32[2048]{0:T(1024)}, u32[]{:S(2)}) copy-start(f32[2048]{0:T(1024)} %param.19) | copy-start | bytes 24580
  169.1 2.3 copy-start.3
  195.3 149.6 %copy-start.10 = (bf16[1,2048,176]{1,2,0:T(8,128)(2,1)S(1)}, bf16[1,2048,176]{1,2,0:T(8,128)(2,1)}, u32[]{:S(2)}) copy-start(bf16[1,2048,176]{1,2,0:T(8,128)(2,1)} %param.23) | copy-start | bytes 2162692
  342.2 2.7 copy-start.4
  344.9 3.0 copy-start.11
  344.9 3.0 copy-start.12
  369.2 58.0 %copy-start.7 = (s32[64,2]{0,1:T(2,128)S(1)}, s32[64,2]{0,1:T(2,128)}, u32[]{:S(2)}) copy-start(s32[64,2]{0,1:T(2,128)} %param.27) | copy-start | bytes 1540
  416.2 35.9 %all-to-all-start.3 = ((bf16[32,6,2048]{2,1,0:T(8,128)(2,1)}), bf16[32,6,2048]{2,1,0:T(8,128)(2,1)S(1)}, u32[]{:S(2)}, u32[]{:S(2)}) async-start(bf16[32,6,2048]{2,1,0:T(8,128)(2,1)} %copy.58), calls=%async_computation.4 | async-start | bytes 2097152 | tf_op jit(solution)/shard_map/all_to_all | solution.py:93
  426.4 99.1 %reduce-scatter.5.cloned.1.call-start = ((), (), s32[]{:S(2)}) async-start(), calls=%async_computation.9 | async-start | bytes 2359296 | tf_op jit(solution)/shard_map/reduce_scatter | solution.py:104
  483.6 43.7 %copy-start.1 = (bf16[4608,256]{1,0:T(8,128)(2,1)S(1)}, bf16[4608,256]{1,0:T(8,128)(2,1)}, u32[]{:S(2)}) copy-start(bf16[4608,256]{1,0:T(8,128)(2,1)} %param.17) | copy-start | bytes 7077892
Sparse Core Ops, SparseCore 0:
  36.8 25.3 all-gather.8
  64.0 28.2 all-gather.6
  94.7 67.9 all-reduce.2
  369.3 44.3 reduce-scatter.2
  491.2 34.2 reduce-scatter.4
where the time goes:
time: 541 us; the launch traced here: 534 us
  blocking collectives  196 us (36%)
  waiting for transfers between devices  176 us (33%)
  local copies, waits for them, and re-layouts  66.2 us (12%)
  other arithmetic  35 us (6%)
  matrix products  30.3 us (6%)
  starting transfers between devices  16.3 us (3%)
  between operations  14.5 us (3%)
    all_to_all x1, blocking collectives, shards(): slots = lax.all_to_all(send, 'dp', split_axis=0, concat_axis=0, tiled=True)  147 us
    psum x1, waiting for transfers between devices, shards(): projected = lax.psum(partial_value.astype(jnp.bfloat16), 'expert')  70.3 us
    reduce_scatter x1, waiting for transfers between devices, shards(): lax.psum_scatter(partial_out.astype(jnp.bfloat16), 'expert', scatter_dime...  44.5 us
    reduce_scatter x1, waiting for transfers between devices, shards(): lax.psum_scatter((jnp.dot(shared_hidden, shared_down, preferred_element_t...  34.4 us
    unnamed x34, local copies, waits for them, and re-layouts  26 us
    all_to_all x1, blocking collectives, shards(): lax.all_to_all(sorted_feats, 'dp', split_axis=0, concat_axis=0, tiled=True)  23.1 us
    reduce_sum x1, other arithmetic, shards(): jnp.sum((picked.astype(jnp.float32) * coef[:, None]).reshape(group_rows,...  15.5 us
    all_to_all x1, waiting for transfers between devices, shards(): lax.all_to_all(summed, 'dp', split_axis=0, concat_axis=0, tiled=True)  13.1 us
  transfers between devices with their start and end apart: 7, of which 5 were waited for; matrix products, arithmetic and copies ran while one was open for 4% of the time, Pallas kernels for 0%

commit v1 on v0

--- a/solution.py
+++ b/solution.py
@@ -59,7 +59,9 @@
         lax.all_gather(route_wts, "expert", axis=0, tiled=True),
     )
     partial_value = project_part(feats, proj_in, proj_out)
-    projected = lax.psum(partial_value.astype(jnp.bfloat16), "expert")
+    block = partial_value.astype(jnp.bfloat16)
+    parts = lax.all_gather(block, "expert")
+    projected = jnp.sum(parts, axis=0)
     block_start = jnp.arange(offsets.shape[0], dtype=jnp.int32) // img_dev * tok_dev
     embed_group = texts.at[offsets + block_start].set(projected)
     normed = normalize(embed_group, norm_gain)

time: 541 us -> 530 us (0.980)
  waiting for transfers between devices: 176 us -> 153 us
    psum x1 -> x0, waiting for transfers between devices: 70.3 us -> none  [shards(): projected = lax.psum(partial_value.astype(jnp.bfloat16), 'expert')]
    all_gather x1, waiting for transfers between devices: 0.02 us -> 25.4 us  [shards(): lax.all_gather(moved_feats, 'expert', axis=0, tiled=True)]
    all_gather x1, waiting for transfers between devices: 12.6 us -> 24.7 us  [shards(): lax.all_gather(text_embed, 'expert', axis=0, tiled=True)]
    all_gather x0 -> x1, waiting for transfers between devices: none -> 11.6 us  [shards(): parts = lax.all_gather(block, 'expert')]
  transfers between devices with their start and end apart: 7 -> 7, of which waited for: 5 -> 6; matrix products, arithmetic and copies ran while one was open for 4% -> 4% of each run, Pallas kernels for 0% -> 0%
where the time goes in v1:
time: 530 us; the launch traced here: 521 us
  blocking collectives  197 us (37%)
  waiting for transfers between devices  153 us (29%)
  local copies, waits for them, and re-layouts  65.4 us (12%)
  other arithmetic  40.2 us (8%)
  matrix products  30.4 us (6%)
  starting transfers between devices  20.7 us (4%)
  between operations  14.4 us (3%)
    all_to_all x1, blocking collectives, shards(): slots = lax.all_to_all(send, 'dp', split_axis=0, concat_axis=0, tiled=True)  149 us
    reduce_scatter x1, waiting for transfers between devices, shards(): lax.psum_scatter(partial_out.astype(jnp.bfloat16), 'expert', scatter_dime...  42.9 us
    reduce_scatter x1, waiting for transfers between devices, shards(): lax.psum_scatter((jnp.dot(shared_hidden, shared_down, preferred_element_t...  34.4 us
    unnamed x34, local copies, waits for them, and re-layouts  26 us
    all_gather x1, waiting for transfers between devices, shards(): lax.all_gather(moved_feats, 'expert', axis=0, tiled=True)  25.4 us
    all_gather x1, waiting for transfers between devices, shards(): lax.all_gather(text_embed, 'expert', axis=0, tiled=True)  24.7 us
    all_to_all x1, blocking collectives, shards(): lax.all_to_all(sorted_feats, 'dp', split_axis=0, concat_axis=0, tiled=True)  23.1 us
    reduce_sum x1, other arithmetic, shards(): jnp.sum((picked.astype(jnp.float32) * coef[:, None]).reshape(group_rows,...  15.5 us
  transfers between devices with their start and end apart: 7, of which 6 were waited for; matrix products, arithmetic and copies ran while one was open for 4% of the time, Pallas kernels for 0%

profile of v1, /device:TPU:2, one launch (start us, length us, event | category | flops | bytes accessed | tf_op | source)
XLA Modules:
  0.0 521.3 jit_solution(7797983607405214158)
XLA Ops:
  6.5 0.8 and_select_fusion.4
  7.4 1.6 sort.17
  9.0 2.0 gather_fusion.1
  11.0 0.5 broadcast.394
  11.5 0.8 reduce.8
  12.3 0.1 reshape.351
  12.4 23.1 %all_to_all.21 = bf16[32,2,2304]{2,1,0:T(2,128)(2,1)S(1)} all-to-all(bf16[32,2,2304]{2,1,0:T(2,128)(2,1)S(1)} %reshape.351), channel_id=1, replica_groups=mesh['dp'=32,'expert'=8] {'dp'}, dimensions={0} | all-to-all | bytes 589824 | tf_op jit(solution)/shard_map/all_to_all | solution.py:49
  35.5 0.2 reshape.352
  35.8 0.8 copy.50
  36.6 0.0 all-gather.13.cloned.1.call-start
  36.7 25.4 %all-gather.11.cloned.1.call-done = bf16[256,1,4608]{2,0,1:T(8,128)(2,1)} async-done(((bf16[32,1,4608]{2,0,1:T(8,128)(2,1)}), bf16[256,1,4608]{2,0,1:T(8,128)(2,1)}) %all-gather.11.cloned.1.call-update) | async-done | bytes 2359312 | tf_op jit(solution)/shard_map/all_gather | solution.py:56
  62.1 4.7 convolution_convert_fusion.1
  66.8 0.7 all-gather.9.cloned.1.call-update
  67.5 0.7 gather_fusion
  68.2 0.7 copy.48
  68.9 10.1 %all-to-all-start = ((s32[32,1,1]{2,1,0:T(1,128)}), s32[32,1,1]{2,1,0:T(1,128)S(1)}, u32[]{:S(2)}, u32[]{:S(2)}) async-start(s32[32,1,1]{2,1,0:T(1,128)} %copy.48), calls=%async_computation | async-start | bytes 32768 | tf_op jit(solution)/shard_map/all_to_all | solution.py:50
  79.1 0.0 reduce-scatter.3.cloned.1.call-start
  79.1 9.4 %all-gather.3 = s32[8,64,2]{1,2,0:T(2,128)S(1)} all-gather(s32[1,64,2]{1,2,0:T(2,128)S(1)} %bitcast.72), channel_id=1, replica_groups=mesh['dp'=32,'expert'=8] {'expert'}, dimensions={0}, use_global_device_ids=true | all-gather | bytes 4608 | tf_op jit(solution)/shard_map/all_gather | solution.py:58
  88.6 0.1 copy.53
  88.7 0.2 copy.51
  88.9 0.2 eq.47
  89.0 0.2 reshape.266
  89.3 9.0 %reduce-window.6 = s32[32,8,128]{2,1,0:T(8,128)S(1)} reduce-window(s32[32,8,128]{2,1,0:T(8,128)S(1)} %fusion.38, s32[]{:T(128)} %constant.100.clone.1), window={size=1x1x128 pad=0_0x0_0x127_0}, to_apply=%region_4.5 | reduce-window | flops 4161536 | bytes 262148 | tf_op jit(solution)/shard_map/reduce-window
  98.3 0.1 slice.16
  98.4 0.1 copy.55
  98.6 0.1 copy.56
  98.7 0.1 broadcast_add_fusion
  98.9 0.1 multiply_reduce_fusion.1
  99.0 0.1 and_reduce_fusion
  99.1 0.6 dynamic-slice
  100.4 0.7 reduce.4
  101.1 0.2 dynamic-update-slice
  101.3 7.0 %all-reduce = s32[256]{0:T(256)S(1)} all-reduce(s32[256]{0:T(256)S(1)} %dynamic-update-slice), channel_id=2, replica_groups=mesh['dp'=32,'expert'=8] {'expert'}, use_global_device_ids=true, to_apply=%add | all-reduce | flops 256 | bytes 2048 | tf_op jit(solution)/shard_map/all_gather | solution.py:57
  108.3 11.6 %all-gather.13.cloned.1.call-done = bf16[2048,2048]{1,0:T(8,128)(2,1)} async-done(((bf16[256,2048]{1,0:T(8,128)(2,1)}), bf16[2048,2048]{1,0:T(8,128)(2,1)}) %all-gather.13.cloned.1.call-update) | async-done | bytes 8388624 | tf_op jit(solution)/shard_map/all_gather | solution.py:63
  119.9 5.2 reduce_sum.48
  125.1 24.7 %all-gather.9.cloned.1.call-done = bf16[512,2048]{1,0:T(8,128)(2,1)} async-done(((bf16[64,2048]{1,0:T(8,128)(2,1)}), bf16[512,2048]{1,0:T(8,128)(2,1)}) %all-gather.9.cloned.1.call-update) | async-done | bytes 2097168 | tf_op jit(solution)/shard_map/all_gather | solution.py:55
  149.8 5.8 %scatter_fusion = bf16[512,2048]{1,0:T(8,128)(2,1)} fusion(bf16[512,2048]{1,0:T(8,128)(2,1)} %all-gather.9.cloned.1.call-done, s32[256]{0:T(256)S(1)} %compare_select_fusion.5, bf16[256,2048]{1,0:T(8,128)(2,1)S(1)} %reduce_sum.48), kind=kCustom, calls=%fused_computation.4 | custom fusion | bytes 3146752 | tf_op jit(solution)/shard_map/scatter | solution.py:66
  155.5 2.2 fusion
  157.8 1.9 fusion.2
  159.7 22.1 %scatter_custom_fusion.1 = bf16[1536,2048]{1,0:T(8,128)(2,1)} fusion(s32[1024]{0:T(1024)S(1)} %get-tuple-element.14, bf16[512,2048]{1,0:T(8,128)(2,1)} %fusion.2, s32[1024]{0:T(1024)S(1)} %get-tuple-element.13, bf16[]{:T(256)} %constant.115.clone.1), kind=kCustom, calls=%fused_computation.13 | custom fusion | bytes 6291968
  181.8 149.3 %all_to_all.22 = bf16[32,48,2048]{2,1,0:T(8,128)(2,1)S(1)} all-to-all(bf16[32,48,2048]{2,1,0:T(8,128)(2,1)} %bitcast.62), channel_id=1, replica_groups=mesh['dp'=32,'expert'=8] {'dp'}, dimensions={0} | all-to-all | bytes 12582912 | tf_op jit(solution)/shard_map/all_to_all | solution.py:85
  331.1 2.7 copy-done.4
  333.7 3.0 fusion.13
  336.8 12.3 %convolution_convert_fusion = bf16[32,48,2048]{2,1,0:T(8,128)(2,1)} fusion(f32[32,48,176]{2,1,0:T(8,128)} %fusion.13, bf16[32,48,2048]{2,1,0:T(8,128)(2,1)} %copy-done.4, bf16[1,176,2048]{2,1,0:T(8,128)(2,1)S(1)} %copy-done.11, bf16[1,2048,176]{1,2,0:T(8,128)(2,1)S(1)} %copy-done.12), kind=kOutput, calls=%fused_computation.9 | convolution fusion | flops 2219360256 | bytes 15106048 | tf_op jit(solution)/shard_map/ncf,fd->ncd/dot_general | solution.py:89
  349.1 8.9 %copy.57 = bf16[32,48,2048]{2,0,1:T(8,128)(2,1)} copy(bf16[32,48,2048]{2,1,0:T(8,128)(2,1)} %convolution_convert_fusion) | data formatting | bytes 12582912 | tf_op jit(solution)/shard_map/convert_element_type | solution.py:93
  358.0 42.9 %reduce-scatter.3.cloned.1.call-done = bf16[32,6,2048]{2,0,1:T(8,128)(2,1)} async-done(((bf16[32,48,2048]{2,0,1:T(8,128)(2,1)}), bf16[32,6,2048]{2,0,1:T(8,128)(2,1)}) %reduce-scatter.3.cloned.1.call-update) | async-done | bytes 786448 | tf_op jit(solution)/shard_map/reduce_scatter | solution.py:92
  400.9 2.6 copy.58
  403.5 10.2 %all-to-all-start.3 = ((bf16[32,6,2048]{2,1,0:T(8,128)(2,1)}), bf16[32,6,2048]{2,1,0:T(8,128)(2,1)S(1)}, u32[]{:S(2)}, u32[]{:S(2)}) async-start(bf16[32,6,2048]{2,1,0:T(8,128)(2,1)} %copy.58), calls=%async_computation.4 | async-start | bytes 2097152 | tf_op jit(solution)/shard_map/all_to_all | solution.py:95
  413.7 0.3 reduce-scatter.5.cloned.1.call-start
  413.9 0.2 div.94
  414.1 0.3 and.78
  414.4 8.6 %all-gather.4 = s32[8,64,2]{1,2,0:T(2,128)S(1)} all-gather(s32[1,64,2]{1,2,0:T(2,128)S(1)} %bitcast.73), channel_id=1, replica_groups=mesh['dp'=32,'expert'=8] {'expert'}, dimensions={0}, use_global_device_ids=true | all-gather | bytes 4608 | tf_op jit(solution)/shard_map/all_gather | solution.py:59
  423.1 0.2 copy.61
  423.2 0.1 reshape.340
  423.3 0.1 fusion.31
  423.5 2.9 fusion.50
  426.4 13.1 %all-to-all-done.3 = bf16[32,6,2048]{2,1,0:T(8,128)(2,1)S(1)} async-done(((bf16[32,6,2048]{2,1,0:T(8,128)(2,1)}), bf16[32,6,2048]{2,1,0:T(8,128)(2,1)S(1)}, u32[]{:S(2)}, u32[]{:S(2)}) %all-to-all-start.3) | async-done | bytes 786464 | tf_op jit(solution)/shard_map/all_to_all | solution.py:95
  439.5 0.3 reshape.268
  439.7 6.1 %gather_fusion.2 = bf16[1024,2048]{1,0:T(8,128)(2,1)} fusion(bf16[192,2048]{1,0:T(8,128)(2,1)S(1)} %reshape.268, s32[1024]{0:T(1024)S(1)} %broadcast_clamp_fusion), kind=kCustom, calls=%fused_computation.3 | custom fusion | bytes 8392704 | tf_op jit(solution)/shard_map/gather | solution.py:98
  445.8 9.6 %reshape.273 = f32[512,2,2048]{2,1,0:T(2,128)} reshape(bf16[1024,2048]{1,0:T(8,128)(2,1)} %gather_fusion.2) | data formatting | bytes 12582912 | tf_op jit(solution)/shard_map/convert_element_type | solution.py:103
  455.5 15.5 %multiply_reduce_fusion = f32[512,2048]{1,0:T(8,128)} fusion(f32[512,2,2048]{2,1,0:T(2,128)} %reshape.273, f32[512,2]{1,0:T(8,128)S(1)} %fusion.31), kind=kLoop, calls=%fused_computation.6 | loop fusion | flops 3145728 | bytes 12587008 | tf_op jit(solution)/shard_map/reduce_sum | solution.py:102
  470.9 7.4 %add_convert_fusion = bf16[512,2048]{1,0:T(8,128)(2,1)} fusion(f32[512,2048]{1,0:T(8,128)} %multiply_reduce_fusion, bf16[352,2048]{1,0:T(8,128)(2,1)} %param.22, bf16[512,2048]{1,0:T(8,128)(2,1)} %fusion.2, bf16[2048,352]{0,1:T(8,128)(2,1)} %param.21, f32[512,352]{0,1:T(8,128)S(1)} %fusion.50), kind=kOutput, calls=%fused_computation.15 | convolution fusion | flops 1479573504 | bytes 11993088 | tf_op jit(solution)/shard_map/dot_general | solution.py:107
  478.4 34.4 %reduce-scatter.5.cloned.1.call-done = bf16[64,2048]{1,0:T(8,128)(2,1)} async-done(((bf16[512,2048]{1,0:T(8,128)(2,1)}), bf16[64,2048]{1,0:T(8,128)(2,1)}) %reduce-scatter.5.cloned.1.call-update) | async-done | bytes 262160 | tf_op jit(solution)/shard_map/reduce_scatter | solution.py:106
  512.7 1.8 add_convert_fusion.1
  (54 shorter events, 0.5 us)
Async XLA Ops:
  6.5 55.5 %copy-start = (bf16[4608,256]{1,0:T(8,128)(2,1)S(1)}, bf16[4608,256]{1,0:T(8,128)(2,1)}, u32[]{:S(2)}) copy-start(bf16[4608,256]{1,0:T(8,128)(2,1)} %param.17) | copy-start | bytes 7077892
  6.5 55.5 %all-gather.11.cloned.1.call-start = ((), (), s32[]{:S(2)}) async-start(), calls=%async_computation.9 | async-start | bytes 2654208 | tf_op jit(solution)/shard_map/all_gather | solution.py:56
  36.6 30.9 %copy-start.2 = (s32[32]{0:T(128)S(1)}, s32[32]{0:T(128)}, u32[]{:S(2)}) copy-start(s32[32]{0:T(128)} %param.16) | copy-start | bytes 388
  36.6 42.5 %copy-start.6 = (s32[64,2]{0,1:T(2,128)S(1)}, s32[64,2]{0,1:T(2,128)}, u32[]{:S(2)}) copy-start(s32[64,2]{0,1:T(2,128)} %param.26) | copy-start | bytes 1540
  36.6 83.3 %all-gather.13.cloned.1.call-start = ((), (), s32[]{:S(2)}) async-start(), calls=%async_computation.10 | async-start | bytes 9437184 | tf_op jit(solution)/shard_map/all_gather | solution.py:63
  66.7 32.2 %copy-start.9 = (s32[2]{0:T(128)S(1)}, s32[2]{0:T(128)}, u32[]{:S(2)}) copy-start(s32[2]{0:T(128)} %constant.130) | copy-start | bytes 28
  66.7 32.3 %copy-start.8 = (s32[2]{0:T(128)S(1)}, s32[2]{0:T(128)}, u32[]{:S(2)}) copy-start(s32[2]{0:T(128)} %constant.133) | copy-start | bytes 28
  66.8 32.4 %copy-start.13 = (u32[256]{0:T(256)S(1)}, u32[256]{0:T(256)}, u32[]{:S(2)}) copy-start(u32[256]{0:T(256)} %constant.140) | copy-start | bytes 3076
  66.8 83.0 %all-gather.9.cloned.1.call-start = ((), (), s32[]{:S(2)}) async-start(), calls=%async_computation.6 | async-start | bytes 2359296 | tf_op jit(solution)/shard_map/all_gather | solution.py:55
  68.9 31.5 %all-to-all-start = ((s32[32,1,1]{2,1,0:T(1,128)}), s32[32,1,1]{2,1,0:T(1,128)S(1)}, u32[]{:S(2)}, u32[]{:S(2)}) async-start(s32[32,1,1]{2,1,0:T(1,128)} %copy.48), calls=%async_computation | async-start | bytes 32768 | tf_op jit(solution)/shard_map/all_to_all | solution.py:50
  79.1 321.8 %reduce-scatter.3.cloned.1.call-start = ((), (), s32[]{:S(2)}) async-start(), calls=%async_computation.7 | async-start | bytes 7077888 | tf_op jit(solution)/shard_map/reduce_scatter | solution.py:92
  125.1 32.7 %copy-start.5 = (f32[2048]{0:T(1024)S(1)}, f32[2048]{0:T(1024)}, u32[]{:S(2)}) copy-start(f32[2048]{0:T(1024)} %param.19) | copy-start | bytes 24580
  155.5 2.3 copy-start.3
  181.8 152.0 %copy-start.10 = (bf16[1,2048,176]{1,2,0:T(8,128)(2,1)S(1)}, bf16[1,2048,176]{1,2,0:T(8,128)(2,1)}, u32[]{:S(2)}) copy-start(bf16[1,2048,176]{1,2,0:T(8,128)(2,1)} %param.23) | copy-start | bytes 2162692
  331.1 2.7 copy-start.4
  333.7 3.0 copy-start.11
  333.7 3.0 copy-start.12
  358.0 56.4 %copy-start.7 = (s32[64,2]{0,1:T(2,128)S(1)}, s32[64,2]{0,1:T(2,128)}, u32[]{:S(2)}) copy-start(s32[64,2]{0,1:T(2,128)} %param.27) | copy-start | bytes 1540
  403.5 36.0 %all-to-all-start.3 = ((bf16[32,6,2048]{2,1,0:T(8,128)(2,1)}), bf16[32,6,2048]{2,1,0:T(8,128)(2,1)S(1)}, u32[]{:S(2)}, u32[]{:S(2)}) async-start(bf16[32,6,2048]{2,1,0:T(8,128)(2,1)} %copy.58), calls=%async_computation.4 | async-start | bytes 2097152 | tf_op jit(solution)/shard_map/all_to_all | solution.py:95
  413.7 99.1 %reduce-scatter.5.cloned.1.call-start = ((), (), s32[]{:S(2)}) async-start(), calls=%async_computation.8 | async-start | bytes 2359296 | tf_op jit(solution)/shard_map/reduce_scatter | solution.py:106
  470.9 43.6 %copy-start.1 = (bf16[4608,256]{1,0:T(8,128)(2,1)S(1)}, bf16[4608,256]{1,0:T(8,128)(2,1)}, u32[]{:S(2)}) copy-start(bf16[4608,256]{1,0:T(8,128)(2,1)} %param.17) | copy-start | bytes 7077892
Sparse Core Ops, SparseCore 0:
  36.7 25.3 all-gather.10
  66.9 52.9 all-gather.12
  121.8 27.9 all-gather.8
  358.1 42.7 reduce-scatter.2
  478.5 34.1 reduce-scatter.4
